TPU v7x, 256 devices: a whole 4x4x8 slice. The times are simulated.
256 devices in a mesh: dp: 8 (over x, core), ctx: 32 (over y, z).
Axes of the slice: x: 4, y: 4, z: 8, core: 2. Of those that a mesh axis runs over, the one named last changes fastest.
Arguments:
- tokens: bfloat16 [32768, 4096], P(('dp', 'ctx')), parts along dimension 0, may hold values from -6 to 6
- pick_flags: int32 [32768], P(('dp', 'ctx')), parts along dimension 0, may hold values from 0 to 1, as said below
- gate_scales: bfloat16 [32768], P(('dp', 'ctx')), parts along dimension 0, may hold values from 0.099609375 to 1
- attn_gain: float32 [4096], replicated, may hold values from 0.4 to 1.6
- query_weight: bfloat16 [4096, 4096], P(None, 'ctx')
- key_weight: bfloat16 [4096, 1024], P(None, 'ctx')
- value_matrix: bfloat16 [4096, 1024], P(None, 'ctx'), may hold values from -0.09375 to 0.09375
- output_weight: bfloat16 [4096, 4096], P('ctx'), may hold values from -0.09375 to 0.09375
- ffn_gain: float32 [4096], replicated, may hold values from 0.25 to 1.75
- gate_weight: bfloat16 [4096, 11264], P(None, 'ctx'), may hold values from -0.09375 to 0.09375
- up_weight: bfloat16 [4096, 11264], P(None, 'ctx'), may hold values from -0.09375 to 0.09375
- down_weight: bfloat16 [11264, 4096], P('ctx'), may hold values from -0.0546875 to 0.0546875
Outputs:
- block_out: bfloat16 [32768, 4096], P(('dp', 'ctx')), parts along dimension 0
There are 8 independent parts, one for each index of `dp`. A program takes and returns all parts, laid end to end along the dimension named above; an argument that names none is the same for every part. Nothing has to cross between parts.
Inputs may be any that keep to these rules, and one draw needn't show every extreme that they name: `pick_flags`: each device's 128 tokens hold at most 32 picks, the first device exactly 32; each document holds exactly 512 picks; a device may hold none.
All inputs are finite; a program needn't handle non-finite values.
Results may differ from a plain program's by a relative error of at most 0.01.
Values may be sent and summed in bfloat16 or wider, within the bound.
A program may use at most 128 MiB of HBM per device.

v0:
```python
import functools

import jax
import jax.numpy as jnp
from jax import lax
from jax.experimental import pallas as pl
from jax.experimental.pallas import tpu as pltpu
from jax.sharding import Mesh, PartitionSpec as P

QUERY_HEADS = 32
KEY_VALUE_HEADS = 8
HEAD_SIZE = 128
PICK_DEV = 16
MOST = 32
Z_RUN = 8
GROUP = ("cy", "cz")


norm_eps = 1e-05
rope_base = 500000.0


def rms_scale(matrix, gain_vec):
    mean_square = jnp.mean(matrix * matrix, axis=-1, keepdims=True)
    return matrix * lax.rsqrt(mean_square + norm_eps) * gain_vec


def apply_rotary(values, token_positions):
    half_dim = values.shape[-1] // 2
    frequency = rope_base ** (-(jnp.arange(half_dim, dtype=jnp.float32) * 2.0) / values.shape[-1])
    angles = token_positions.astype(jnp.float32)[:, None] * frequency[None, :]
    cosine = jnp.cos(angles)
    sine_part = jnp.sin(angles)
    lower_half = values[..., :half_dim]
    upper_half = values[..., half_dim:]
    return jnp.concatenate(
        (
            lower_half * cosine - upper_half * sine_part,
            upper_half * cosine + lower_half * sine_part,
        ),
        axis=-1,
    )


MESH_ID = pl.DeviceIdType.MESH
SUB_CHUNKS = 2


def _enter(nz, ny):
    me_z = lax.axis_index("cz")
    me_y = lax.axis_index("cy")
    barrier = pltpu.get_barrier_semaphore()
    for neighbour in (lax.rem(me_z + nz - 1, nz), lax.rem(me_z + 1, nz)):
        pl.semaphore_signal(barrier, inc=1, device_id={"cz": neighbour}, device_id_type=MESH_ID)
    for shift in range(1, ny):
        pl.semaphore_signal(barrier, inc=1, device_id={"cy": lax.rem(me_y + shift, ny)}, device_id_type=MESH_ID)
    pl.semaphore_wait(barrier, 2 + ny - 1)
    return me_z, me_y


def _rs_kernel(n, ny, a_ref, w_ref, out_ref, recv, sendbuf, firstbuf, send_sem, recv_sem, zsum, ybuf, yrecv, ysend_sem, yrecv_sem):
    me, me_y = _enter(n, ny)
    right = lax.rem(me + 1, n)
    left = lax.rem(me + n - 1, n)
    half = w_ref.shape[1] // 2
    piece = a_ref.shape[1] // SUB_CHUNKS
    own = out_ref.shape[0]
    dest = (right, left)

    def part(chunk, k, d):
        return jnp.dot(
            a_ref[chunk, pl.ds(k * piece, piece), :],
            w_ref[:, pl.ds(d * half, half)],
            preferred_element_type=jnp.float32,
        ).astype(sendbuf.dtype)

    def link(d, slot, k, src):
        return pltpu.make_async_remote_copy(
            src_ref=src,
            dst_ref=recv.at[d, slot, k],
            send_sem=send_sem.at[d, slot, k],
            recv_sem=recv_sem.at[d, slot, k],
            device_id={"cz": dest[d]},
            device_id_type=MESH_ID,
        )

    sends = []
    for k in range(SUB_CHUNKS):
        for d in range(2):
            first = lax.rem(me + n - 1, n) if d == 0 else lax.rem(me + 1, n)
            firstbuf[d, k] = part(first, k, d)
            copy = link(d, 0, k, firstbuf.at[d, k])
            copy.start()
            sends.append(copy)
    for step in range(n - 1):
        for k in range(SUB_CHUNKS):
            for d in range(2):
                if d == 0:
                    chunk = lax.rem(me + 2 * n - step - 2, n)
                else:
                    chunk = lax.rem(me + step + 2, n)
                mine = part(chunk, k, d).astype(jnp.float32)
                link(d, step, k, sendbuf.at[d, step, k]).wait_recv()
                total = recv[d, step, k].astype(jnp.float32) + mine
                if step == n - 2:
                    zsum[pl.ds(k * piece, piece), pl.ds(d * half, half)] = total
                else:
                    sendbuf[d, step, k] = total.astype(sendbuf.dtype)
                    copy = link(d, step + 1, k, sendbuf.at[d, step, k])
                    copy.start()
                    sends.append(copy)
    ysends = []
    for shift in range(1, ny):
        peer = lax.rem(me_y + shift, ny)
        ybuf[shift - 1] = zsum[pl.ds(pl.multiple_of(peer * own, own), own), :].astype(ybuf.dtype)
        copy = pltpu.make_async_remote_copy(
            src_ref=ybuf.at[shift - 1],
            dst_ref=yrecv.at[shift - 1],
            send_sem=ysend_sem.at[shift - 1],
            recv_sem=yrecv_sem.at[shift - 1],
            device_id={"cy": peer},
            device_id_type=MESH_ID,
        )
        copy.start()
        ysends.append(copy)
    total = zsum[pl.ds(pl.multiple_of(me_y * own, own), own), :]
    for shift in range(1, ny):
        ysends[shift - 1].wait_recv()
        total = total + yrecv[shift - 1].astype(jnp.float32)
    out_ref[...] = total
    for copy in sends + ysends:
        copy.wait_send()


def reduce_scatter_kernel(a, w, ny, collective_id):
    n, rows, _ = a.shape
    cols = w.shape[1]
    half = cols // 2
    piece = rows // SUB_CHUNKS
    own = rows // ny
    return pl.pallas_call(
        functools.partial(_rs_kernel, n, ny),
        out_shape=jax.ShapeDtypeStruct((own, cols), jnp.float32),
        in_specs=[pl.BlockSpec(memory_space=pltpu.VMEM), pl.BlockSpec(memory_space=pltpu.VMEM)],
        out_specs=pl.BlockSpec(memory_space=pltpu.VMEM),
        scratch_shapes=[
            pltpu.VMEM((2, n - 1, SUB_CHUNKS, piece, half), w.dtype),
            pltpu.VMEM((2, n - 1, SUB_CHUNKS, piece, half), w.dtype),
            pltpu.VMEM((2, SUB_CHUNKS, piece, half), w.dtype),
            pltpu.SemaphoreType.DMA((2, n - 1, SUB_CHUNKS)),
            pltpu.SemaphoreType.DMA((2, n - 1, SUB_CHUNKS)),
            pltpu.VMEM((rows, cols), jnp.float32),
            pltpu.VMEM((ny - 1, own, cols), w.dtype),
            pltpu.VMEM((ny - 1, own, cols), w.dtype),
            pltpu.SemaphoreType.DMA((ny - 1,)),
            pltpu.SemaphoreType.DMA((ny - 1,)),
        ],
        compiler_params=pltpu.CompilerParams(collective_id=collective_id, has_side_effects=True),
    )(a, w)


def _ag_kernel(n, ny, x_ref, out_ref, own_sem, ysend_sem, yrecv_sem, send_sem, recv_sem):
    me, me_y = _enter(n, ny)
    right = lax.rem(me + 1, n)
    left = lax.rem(me + n - 1, n)
    rows = x_ref.shape[0]
    half = rows // 2
    dest = (right, left)
    mine = pltpu.make_async_copy(x_ref, out_ref.at[me, me_y], own_sem.at[0])
    mine.start()
    ysends = []
    for shift in range(1, ny):
        peer = lax.rem(me_y + shift, ny)
        copy = pltpu.make_async_remote_copy(
            src_ref=x_ref,
            dst_ref=out_ref.at[me, me_y],
            send_sem=ysend_sem.at[shift - 1],
            recv_sem=yrecv_sem.at[me_y],
            device_id={"cy": peer},
            device_id_type=MESH_ID,
        )
        copy.start()
        ysends.append(copy)
    mine.wait()
    for shift in range(1, ny):
        peer = lax.rem(me_y + shift, ny)
        pltpu.make_async_remote_copy(
            src_ref=x_ref,
            dst_ref=out_ref.at[me, peer],
            send_sem=ysend_sem.at[shift - 1],
            recv_sem=yrecv_sem.at[peer],
            device_id={"cy": peer},
            device_id_type=MESH_ID,
        ).wait_recv()

    def link(d, step, k, idx):
        rows_here = pl.ds(d * half, half)
        blocks = pl.ds(k * (ny // SUB_CHUNKS), ny // SUB_CHUNKS)
        return pltpu.make_async_remote_copy(
            src_ref=out_ref.at[idx, blocks, rows_here],
            dst_ref=out_ref.at[idx, blocks, rows_here],
            send_sem=send_sem.at[d, step, k],
            recv_sem=recv_sem.at[d, step, k],
            device_id={"cz": dest[d]},
            device_id_type=MESH_ID,
        )

    sends = []
    for step in range(n - 1):
        for k in range(SUB_CHUNKS):
            for d in range(2):
                if step > 0:
                    got = lax.rem(me + n - step, n) if d == 0 else lax.rem(me + step, n)
                    link(d, step - 1, k, got).wait_recv()
                idx = lax.rem(me + n - step, n) if d == 0 else lax.rem(me + step, n)
                copy = link(d, step, k, idx)
                copy.start()
                sends.append(copy)
    for k in range(SUB_CHUNKS):
        for d in range(2):
            got = lax.rem(me + 1, n) if d == 0 else lax.rem(me + n - 1, n)
            link(d, n - 2, k, got).wait_recv()
    for copy in ysends + sends:
        copy.wait_send()


def all_gather_kernel(x, n, ny, collective_id):
    rows, cols = x.shape
    out = pl.pallas_call(
        functools.partial(_ag_kernel, n, ny),
        out_shape=jax.ShapeDtypeStruct((n, ny, rows, cols), x.dtype),
        in_specs=[pl.BlockSpec(memory_space=pltpu.VMEM)],
        out_specs=pl.BlockSpec(memory_space=pltpu.VMEM),
        scratch_shapes=[
            pltpu.SemaphoreType.DMA((1,)),
            pltpu.SemaphoreType.DMA((ny - 1,)),
            pltpu.SemaphoreType.DMA((ny,)),
            pltpu.SemaphoreType.DMA((2, n - 1, SUB_CHUNKS)),
            pltpu.SemaphoreType.DMA((2, n - 1, SUB_CHUNKS)),
        ],
        compiler_params=pltpu.CompilerParams(collective_id=collective_id, has_side_effects=True),
    )(x)
    return out.reshape(n * ny * rows, cols)


def _ag2_kernel(n, ny, x_ref, out1, out2, own_sem, y1_send, y1_recv, z1_send, z1_recv, z2_send, z2_recv, y2_send, y2_recv):
    me, me_y = _enter(n, ny)
    right = lax.rem(me + 1, n)
    left = lax.rem(me + n - 1, n)
    r = out1.shape[2]
    half = r // 2
    dest = (right, left)
    mine1 = pltpu.make_async_copy(x_ref.at[pl.ds(0, r)], out1.at[me, me_y], own_sem.at[0])
    mine2 = pltpu.make_async_copy(x_ref.at[pl.ds(r, r)], out2.at[me_y, me], own_sem.at[1])
    mine1.start()
    mine2.start()

    def to_y(shift, src, dst, send_sem, recv_sem, sender):
        peer = lax.rem(me_y + shift, ny)
        return pltpu.make_async_remote_copy(
            src_ref=src,
            dst_ref=dst,
            send_sem=send_sem.at[shift - 1],
            recv_sem=recv_sem.at[sender],
            device_id={"cy": peer},
            device_id_type=MESH_ID,
        )

    sends = []
    for shift in range(1, ny):
        copy = to_y(shift, x_ref.at[pl.ds(0, r)], out1.at[me, me_y], y1_send, y1_recv, me_y)
        copy.start()
        sends.append(copy)

    def ring2(d, step, idx, src=None):
        rows_here = pl.ds(d * half, half)
        return pltpu.make_async_remote_copy(
            src_ref=out2.at[me_y, idx, rows_here] if src is None else src,
            dst_ref=out2.at[me_y, idx, rows_here],
            send_sem=z2_send.at[d, step],
            recv_sem=z2_recv.at[d, step],
            device_id={"cz": dest[d]},
            device_id_type=MESH_ID,
        )

    for step in range(n - 1):
        for d in range(2):
            idx = lax.rem(me + n - step, n) if d == 0 else lax.rem(me + step, n)
            if step == 0:
                copy = ring2(d, 0, idx, x_ref.at[pl.ds(r + d * half, half)])
            else:
                ring2(d, step - 1, idx).wait_recv()
                copy = ring2(d, step, idx)
            copy.start()
            sends.append(copy)
    for d in range(2):
        got = lax.rem(me + 1, n) if d == 0 else lax.rem(me + n - 1, n)
        ring2(d, n - 2, got).wait_recv()
    mine2.wait()
    ysends2 = []
    for shift in range(1, ny):
        copy = to_y(shift, out2.at[me_y], out2.at[me_y], y2_send, y2_recv, me_y)
        copy.start()
        ysends2.append(copy)

    mine1.wait()
    for shift in range(1, ny):
        peer = lax.rem(me_y + shift, ny)
        to_y(shift, x_ref.at[pl.ds(0, r)], out1.at[me, peer], y1_send, y1_recv, peer).wait_recv()

    def ring1(d, step, idx):
        rows_here = pl.ds(d * half, half)
        return pltpu.make_async_remote_copy(
            src_ref=out1.at[idx, :, rows_here],
            dst_ref=out1.at[idx, :, rows_here],
            send_sem=z1_send.at[d, step],
            recv_sem=z1_recv.at[d, step],
            device_id={"cz": dest[d]},
            device_id_type=MESH_ID,
        )

    for step in range(n - 1):
        for d in range(2):
            if step > 0:
                got = lax.rem(me + n - step, n) if d == 0 else lax.rem(me + step, n)
                ring1(d, step - 1, got).wait_recv()
            idx = lax.rem(me + n - step, n) if d == 0 else lax.rem(me + step, n)
            copy = ring1(d, step, idx)
            copy.start()
            sends.append(copy)
    for d in range(2):
        got = lax.rem(me + 1, n) if d == 0 else lax.rem(me + n - 1, n)
        ring1(d, n - 2, got).wait_recv()
    for shift in range(1, ny):
        peer = lax.rem(me_y + shift, ny)
        to_y(shift, out2.at[me_y], out2.at[peer], y2_send, y2_recv, peer).wait_recv()
    for copy in sends + ysends2:
        copy.wait_send()


def all_gather_two_way(x, n, ny, collective_id):
    rows, cols = x.shape
    r = rows // 2
    out1, out2 = pl.pallas_call(
        functools.partial(_ag2_kernel, n, ny),
        out_shape=(
            jax.ShapeDtypeStruct((n, ny, r, cols), x.dtype),
            jax.ShapeDtypeStruct((ny, n, r, cols), x.dtype),
        ),
        in_specs=[pl.BlockSpec(memory_space=pltpu.VMEM)],
        out_specs=(pl.BlockSpec(memory_space=pltpu.VMEM), pl.BlockSpec(memory_space=pltpu.VMEM)),
        scratch_shapes=[
            pltpu.SemaphoreType.DMA((2,)),
            pltpu.SemaphoreType.DMA((ny - 1,)),
            pltpu.SemaphoreType.DMA((ny,)),
            pltpu.SemaphoreType.DMA((2, n - 1)),
            pltpu.SemaphoreType.DMA((2, n - 1)),
            pltpu.SemaphoreType.DMA((2, n - 1)),
            pltpu.SemaphoreType.DMA((2, n - 1)),
            pltpu.SemaphoreType.DMA((ny - 1,)),
            pltpu.SemaphoreType.DMA((ny,)),
        ],
        compiler_params=pltpu.CompilerParams(collective_id=collective_id, has_side_effects=True),
    )(x)
    return out1.reshape(n * ny * r, cols), out2.reshape(ny * n * r, cols)


def body(
    tokens,
    pick_flags,
    gate_scales,
    attn_gain,
    query_weight,
    key_weight,
    value_matrix,
    output_weight,
    ffn_gain,
    gate_weight,
    up_weight,
    down_weight,
):
    tok_local, width = tokens.shape
    y_size = lax.axis_size("cy")
    z_size = lax.axis_size("cz")
    ctx_size = y_size * z_size
    my_index = lax.axis_index("cy") * z_size + lax.axis_index("cz")
    blk = jnp.arange(ctx_size, dtype=jnp.int32)
    block_dev = (blk % y_size) * z_size + blk // y_size
    picked_count = PICK_DEV * ctx_size
    slots = MOST * ctx_size
    half_pick = PICK_DEV // 2
    half_cycle = ctx_size // 2
    slot_of = jnp.cumsum(pick_flags) - 1
    token_ids = jnp.arange(tok_local, dtype=jnp.int32)
    slot_match = (jnp.arange(MOST, dtype=jnp.int32)[:, None] == slot_of[None, :]) & (
        pick_flags[None, :] == 1
    )
    chosen = jnp.sum(jnp.where(slot_match, token_ids[None, :], 0), axis=1)
    filled = jnp.any(slot_match, axis=1)
    local_index = jnp.where(filled, chosen, -1)
    padded_rows = jnp.where(filled[:, None], tokens[chosen], jnp.zeros((), jnp.bfloat16))
    padded_gate = jnp.where(filled, gate_scales[chosen], jnp.zeros((), jnp.bfloat16))
    lane = jnp.arange(128, dtype=jnp.int32)[None, :]
    extra = jnp.where(
        lane == 0,
        local_index.astype(jnp.bfloat16)[:, None],
        jnp.where(lane == 1, padded_gate[:, None], jnp.zeros((), jnp.bfloat16)),
    )
    packed = jnp.concatenate((padded_rows, extra), axis=1)
    lead = MOST // 2
    part_one, part_two = all_gather_two_way(packed, z_size, y_size, 3)
    slot_ids = jnp.arange(slots, dtype=jnp.int32)
    part_blk = (slot_ids % (slots // 2)) // lead
    slot_dev = jnp.where(
        slot_ids < slots // 2, (part_blk % y_size) * z_size + part_blk // y_size, part_blk
    )
    all_index = jnp.concatenate((part_one[:, width], part_two[:, width])).astype(jnp.int32)
    slot_filled = all_index >= 0
    per_part = jnp.sum(slot_filled.reshape(2, ctx_size, lead).astype(jnp.int32), axis=2)
    counts = per_part[0].reshape(z_size, y_size).T.reshape(ctx_size) + per_part[1]
    run_ends = jnp.cumsum(counts)
    run_starts = run_ends - counts
    slot_pos = slot_dev * tok_local + all_index
    rope_pos = jnp.where(slot_filled, slot_pos, 0)
    never = jnp.int32(1 << 30)
    mask_pos = jnp.where(slot_filled, slot_pos, never)
    normalized = jnp.concatenate(
        (
            rms_scale(part_one[:, :width].astype(jnp.float32), attn_gain).astype(jnp.bfloat16),
            rms_scale(part_two[:, :width].astype(jnp.float32), attn_gain).astype(jnp.bfloat16),
        ),
        axis=0,
    )
    queries = jnp.dot(normalized, query_weight, preferred_element_type=jnp.float32)
    queries = apply_rotary(queries, rope_pos).astype(jnp.bfloat16)
    kv_weight = jnp.concatenate((key_weight, value_matrix), axis=1)
    kv_local = jnp.einsum(
        "pd,dc->cp", normalized, kv_weight, preferred_element_type=jnp.float32
    ).astype(jnp.bfloat16)
    comps = key_weight.shape[1] // KEY_VALUE_HEADS
    query_group_width = QUERY_HEADS // KEY_VALUE_HEADS
    by_head = jnp.transpose(kv_local.reshape(2, comps, KEY_VALUE_HEADS, slots), (2, 0, 1, 3))
    send = jnp.repeat(by_head, query_group_width, axis=0)
    got = lax.all_to_all(send, GROUP, 0, 0, tiled=True)
    key_cols = got[:, 0].reshape(ctx_size * comps, slots)
    value_cols = got[:, 1].reshape(ctx_size * comps, slots)
    keys_here = apply_rotary(key_cols.T.astype(jnp.float32), rope_pos).astype(jnp.bfloat16)
    values_here = value_cols.T
    scores = jnp.dot(queries, keys_here.T, preferred_element_type=jnp.float32) / jnp.sqrt(
        jnp.float32(HEAD_SIZE)
    )
    allowed = mask_pos[None, :] <= mask_pos[:, None]
    scores = jnp.where(allowed, scores, -jnp.inf)
    row_max = jnp.max(scores, axis=1, keepdims=True)
    exp_terms = jnp.exp(scores - row_max)
    prob_bf = (exp_terms / jnp.sum(exp_terms, axis=1, keepdims=True)).astype(jnp.bfloat16)
    head_pad = jnp.dot(prob_bf, values_here, preferred_element_type=jnp.float32).astype(jnp.bfloat16)
    order_ids = jnp.arange(picked_count, dtype=jnp.int32)
    owner_of = order_ids // PICK_DEV
    within = order_ids % PICK_DEV
    low_part = within < half_pick
    rank_block = jnp.where(low_part, owner_of, (owner_of + half_cycle) % ctx_size)
    rank_inner = jnp.where(low_part, 2 * within, 2 * (within - half_pick) + 1)
    rank_ids = rank_block * PICK_DEV + rank_inner
    before = (run_ends[None, :] <= rank_ids[:, None]).astype(jnp.int32)
    source = jnp.sum(before, axis=1)
    offset = rank_ids - jnp.sum(before * counts[None, :], axis=1)
    source_block = (source % z_size) * y_size + source // z_size
    flat_row = jnp.where(
        offset < lead, source_block * lead + offset, slots // 2 + source * lead + offset - lead
    )
    flat_blocked = flat_row.reshape(ctx_size, PICK_DEV)[block_dev].reshape(picked_count)
    pick_onehot = (flat_blocked[:, None] == slot_ids[None, :]).astype(jnp.bfloat16)
    head_out = jnp.dot(pick_onehot, head_pad, preferred_element_type=jnp.float32).astype(jnp.bfloat16)
    own_start = my_index * PICK_DEV
    own_flat = lax.dynamic_slice_in_dim(flat_row, own_start, PICK_DEV, 0)
    part_slots = jnp.arange(slots // 2, dtype=jnp.int32)[None, :]
    pick_one = (own_flat[:, None] == part_slots).astype(jnp.bfloat16)
    pick_two = (own_flat[:, None] - slots // 2 == part_slots).astype(jnp.bfloat16)
    own_packed = jnp.dot(pick_one, part_one, preferred_element_type=jnp.float32) + jnp.dot(
        pick_two, part_two, preferred_element_type=jnp.float32
    )
    own_rows = own_packed[:, :width]
    scale_own = own_packed[:, width + 1]
    attn_own = reduce_scatter_kernel(
        head_out.reshape(z_size, y_size * PICK_DEV, head_out.shape[1]), output_weight, y_size, 0
    )
    mixed_own = own_rows + attn_own
    normed_own = rms_scale(mixed_own, ffn_gain).astype(jnp.bfloat16)
    normed_ffn = all_gather_kernel(normed_own, z_size, y_size, 2)
    gate_proj = jnp.dot(normed_ffn, gate_weight, preferred_element_type=jnp.float32)
    up_proj = jnp.dot(normed_ffn, up_weight, preferred_element_type=jnp.float32)
    hidden = (jax.nn.silu(gate_proj) * up_proj).astype(jnp.bfloat16)
    ffn_own = reduce_scatter_kernel(
        hidden.reshape(z_size, y_size * PICK_DEV, hidden.shape[1]), down_weight, y_size, 1
    )
    final_own = (own_rows + scale_own[:, None] * (attn_own + ffn_own)).astype(jnp.bfloat16)
    own_source = lax.dynamic_slice_in_dim(source, own_start, PICK_DEV, 0)
    targets = jnp.arange(ctx_size, dtype=jnp.int32)[:, None]
    first_half = (own_source[None, :half_pick] == targets)[:, :, None]
    second_half = (own_source[None, half_pick:] == targets)[:, :, None]
    zero = jnp.zeros((), jnp.bfloat16)
    back = jnp.where(
        first_half,
        final_own[None, :half_pick],
        jnp.where(second_half, final_own[None, half_pick:], zero),
    )
    returned = lax.all_to_all(back, GROUP, 0, 0, tiled=True).reshape(ctx_size * half_pick, width)
    my_start = run_starts[my_index]
    rank_here = jnp.clip(my_start + slot_of, 0, picked_count - 1)
    inner_here = rank_here % PICK_DEV
    odd_here = inner_here % 2
    owner_here = (rank_here // PICK_DEV + odd_here * half_cycle) % ctx_size
    take_rows = owner_here * half_pick + inner_here // 2
    return jnp.where(pick_flags[:, None] == 1, returned[take_rows], tokens)


def solution(mesh):
    dp_size, ctx_size = mesh.devices.shape
    z_size = Z_RUN if ctx_size % Z_RUN == 0 else ctx_size
    split = Mesh(mesh.devices.reshape(dp_size, ctx_size // z_size, z_size), ("dp", "cy", "cz"))
    rows = ("dp", "cy", "cz")
    in_specs = (
        P(rows, None),
        P(rows),
        P(rows),
        P(),
        P(None, GROUP),
        P(None, GROUP),
        P(None, GROUP),
        P(GROUP, None),
        P(),
        P(None, GROUP),
        P(None, GROUP),
        P(GROUP, None),
    )
    out_specs = P(rows, None)
    return jax.shard_map(body, mesh=split, in_specs=in_specs, out_specs=out_specs, check_vma=False)
```

profile of v0, /device:TPU:32, one launch (start us, length us, event | category | flops | bytes accessed | tf_op | source)
XLA Modules:
  0.0 366.9 jit_solution(14094527797906659803)
XLA Ops:
  3.6 2.3 gather_fusion
  6.8 84.1 %shard_map.118 = (bf16[8,4,16,4224]{3,2,1,0:T(8,128)(2,1)}, bf16[4,8,16,4224]{3,2,1,0:T(8,128)(2,1)}) custom-call(bf16[32,4224]{1,0:T(8,128)(2,1)} %pad_maximum_fusion.5.x_ref), custom_call_target="tpu_custom_call" | custom-call | tf_op jit(solution)/shard_map/pallas_call | solution.py:344
  90.9 3.2 fusion.3
  94.1 3.1 fusion
  97.3 4.7 %fusion.2 = (bf16[512,4096]{1,0:T(8,128)(2,1)S(1)}, bf16[512,4096]{1,0:T(8,128)(2,1)S(1)}) fusion(f32[4096]{0:T(1024)S(1)} %copy-done.9, f32[512]{0:T(512)S(1)} %add_rsqrt_fusion.1, bf16[512,4224]{1,0:T(8,128)(2,1)} %bitcast.41, f32[512]{0:T(512)S(1)} %add_rsqrt_fusion, bf16[512,4224]{1,0:T(8,128)(2,1)S(1)} %bitcast.39), kind=kLoop, calls=%fused_computation.10 | loop fusion | flops 16777216 | bytes 16797696 | tf_op jit(solution)/shard_map/convert_element_type | solution.py:429
  102.0 2.7 fusion.15
  106.3 11.9 %all-to-all-start = ((bf16[32,2,4,1024]{3,2,1,0:T(4,128)(2,1)}), bf16[32,2,4,1024]{3,2,1,0:T(4,128)(2,1)}, u32[]{:S(2)}, u32[]{:S(2)}) async-start(bf16[32,2,4,1024]{3,2,1,0:T(4,128)(2,1)} %bitcast.11), calls=%async_computation | async-start | bytes 1048576 | tf_op jit(solution)/shard_map/all_to_all | solution.py:444
  121.8 2.9 fusion.55
  124.8 2.9 convolution_add_fusion
  128.6 7.4 %fusion.7 = f32[1024,128]{0,1:T(8,128)} fusion(bf16[4096,128]{1,0:T(8,128)(2,1)} %param.16, bf16[512,4096]{1,0:T(8,128)(2,1)} %copy-done.6, bf16[512,4096]{1,0:T(8,128)(2,1)} %copy-done.5), kind=kOutput, calls=%fused_computation.17 | convolution fusion | flops 1090519040 | bytes 9961472 | tf_op jit(solution)/shard_map/dot_general | solution.py:434
  136.0 2.0 slice_convert_fusion
  138.0 2.0 reshape.690
  140.8 2.6 fusion.33
  147.2 4.7 %fusion.14 = bf16[512,128]{1,0:T(8,128)(2,1)} fusion(s32[512]{0:T(512)S(1)} %eq.146, bf16[128,1024]{1,0:T(8,128)(2,1)S(1)} %copy-done.7, f32[1024,1024]{0,1:T(8,128)} %copy-done.3, f32[1024]{0:T(1024)S(1)} %fusion.8, f32[1024]{0:T(1024)S(1)} %get-tuple-element.29, s32[1024]{0:T(1024)S(1)} %get-tuple-element.13), kind=kOutput, calls=%fused_computation.30 | convolution fusion | flops 409665536 | bytes 4601856 | tf_op jit(solution)/shard_map/dot_general | solution.py:474
  152.0 52.0 %shard_map.119 = f32[16,4096]{1,0:T(8,128)} custom-call(bf16[8,64,128]{2,1,0:T(8,128)(2,1)} %bitcast.49, bf16[128,4096]{1,0:T(8,128)(2,1)} %w_ref.2), custom_call_target="tpu_custom_call" | custom-call | tf_op jit(solution)/shard_map/pallas_call | solution.py:141
  206.8 47.5 %shard_map.120 = bf16[8,4,16,4096]{3,2,1,0:T(8,128)(2,1)} custom-call(bf16[16,4096]{1,0:T(8,128)(2,1)} %multiply_convert_fusion.x_ref), custom_call_target="tpu_custom_call" | custom-call | tf_op jit(solution)/shard_map/pallas_call | solution.py:229
  254.4 4.0 %fusion.125 = f32[512,352]{0,1:T(8,128)S(1)} fusion(bf16[512,4096]{1,0:T(8,128)(2,1)} %bitcast.44, bf16[4096,352]{0,1:T(8,128)(2,1)S(1)} %copy-done), kind=kOutput, calls=%fused_computation.252 | convolution fusion | flops 1476395008 | bytes 7798784 | tf_op jit(solution)/shard_map/dot_general | solution.py:491
  258.7 2.5 fusion.12
  261.2 1.9 copy.45
  263.2 56.0 %shard_map.121 = f32[16,4096]{1,0:T(8,128)} custom-call(bf16[8,64,352]{2,1,0:T(8,128)(2,1)} %bitcast.47, bf16[352,4096]{1,0:T(8,128)(2,1)} %w_ref.3), custom_call_target="tpu_custom_call" | custom-call | tf_op jit(solution)/shard_map/pallas_call | solution.py:141
  322.1 7.0 %all-to-all-start.1 = ((bf16[32,8,4096]{2,1,0:T(8,128)(2,1)}), bf16[32,8,4096]{2,1,0:T(8,128)(2,1)}, u32[]{:S(2)}, u32[]{:S(2)}) async-start(bf16[32,8,4096]{2,1,0:T(8,128)(2,1)} %select_select_fusion), calls=%async_computation.1 | async-start | bytes 4194304 | tf_op jit(solution)/shard_map/all_to_all | solution.py:508
  330.7 28.3 %all-to-all-done.1 = bf16[32,8,4096]{2,1,0:T(8,128)(2,1)} async-done(((bf16[32,8,4096]{2,1,0:T(8,128)(2,1)}), bf16[32,8,4096]{2,1,0:T(8,128)(2,1)}, u32[]{:S(2)}, u32[]{:S(2)}) %all-to-all-start.1) | async-done | bytes 2097184 | tf_op jit(solution)/shard_map/all_to_all | solution.py:508
  359.0 5.0 %gather_fusion.3 = bf16[128,4096]{1,0:T(8,128)(2,1)} fusion(bf16[256,4096]{1,0:T(8,128)(2,1)} %bitcast.16, s32[1024]{0:T(1024)S(1)} %pad_clamp_fusion), kind=kCustom, calls=%fused_computation.3 | custom fusion | bytes 2097664 | tf_op jit(solution)/shard_map/gather | solution.py:515
  364.0 2.7 broadcast_select_fusion
  (94 shorter events, 22.7 us)
Async XLA Ops:
  0.0 254.4 %copy-start = (bf16[4096,352]{0,1:T(8,128)(2,1)S(1)}, bf16[4096,352]{0,1:T(8,128)(2,1)}, u32[]{:S(2)}) copy-start(bf16[4096,352]{0,1:T(8,128)(2,1)} %param.21) | copy-start | bytes 8650756
  90.9 6.4 %copy-start.1 = (bf16[4,8,16,4224]{3,2,1,0:T(8,128)(2,1)S(1)}, bf16[4,8,16,4224]{3,2,1,0:T(8,128)(2,1)}, u32[]{:S(2)}) copy-start(bf16[4,8,16,4224]{3,2,1,0:T(8,128)(2,1)} %get-tuple-element.8) | copy-start | bytes 12976132
  90.9 6.4 %copy-start.9 = (f32[4096]{0:T(1024)S(1)}, f32[4096]{0:T(1024)}, u32[]{:S(2)}) copy-start(f32[4096]{0:T(1024)} %param.15) | copy-start | bytes 49156
  97.2 4.7 %copy-start.11 = (bf16[4096,32]{0,1:T(8,128)(2,1)S(1)}, bf16[4096,32]{0,1:T(8,128)(2,1)}, u32[]{:S(2)}) copy-start(bf16[4096,32]{0,1:T(8,128)(2,1)} %param.18) | copy-start | bytes 786436
  97.3 4.7 %copy-start.12 = (bf16[4096,32]{0,1:T(8,128)(2,1)S(1)}, bf16[4096,32]{0,1:T(8,128)(2,1)}, u32[]{:S(2)}) copy-start(bf16[4096,32]{0,1:T(8,128)(2,1)} %param.17) | copy-start | bytes 786436
  101.9 2.7 copy-start.5
  102.0 3.2 copy-start.6
  106.3 29.7 %all-to-all-start = ((bf16[32,2,4,1024]{3,2,1,0:T(4,128)(2,1)}), bf16[32,2,4,1024]{3,2,1,0:T(4,128)(2,1)}, u32[]{:S(2)}, u32[]{:S(2)}) async-start(bf16[32,2,4,1024]{3,2,1,0:T(4,128)(2,1)} %bitcast.11), calls=%async_computation | async-start | bytes 1048576 | tf_op jit(solution)/shard_map/all_to_all | solution.py:444
  143.4 3.8 %copy-start.7 = (bf16[128,1024]{1,0:T(8,128)(2,1)S(1)}, bf16[128,1024]{1,0:T(8,128)(2,1)}, u32[]{:S(2)}) copy-start(bf16[128,1024]{1,0:T(8,128)(2,1)} %reshape_squeeze.8) | copy-start | bytes 786436
  144.2 1.9 copy-start.3
  147.2 57.9 %copy-start.8 = (f32[4096]{0:T(1024)S(1)}, f32[4096]{0:T(1024)}, u32[]{:S(2)}) copy-start(f32[4096]{0:T(1024)} %param.20) | copy-start | bytes 49156
  254.4 4.0 %copy-start.4 = (bf16[8,4,16,4096]{3,2,1,0:T(8,128)(2,1)S(1)}, bf16[8,4,16,4096]{3,2,1,0:T(8,128)(2,1)}, u32[]{:S(2)}) copy-start(bf16[8,4,16,4096]{3,2,1,0:T(8,128)(2,1)} %shard_map.120) | copy-start | bytes 12582916
  254.4 4.3 %copy-start.10 = (bf16[4096,352]{0,1:T(8,128)(2,1)S(1)}, bf16[4096,352]{0,1:T(8,128)(2,1)}, u32[]{:S(2)}) copy-start(bf16[4096,352]{0,1:T(8,128)(2,1)} %param.22) | copy-start | bytes 8650756
  261.2 58.0 %copy-start.2 = (f32[16,4096]{1,0:T(8,128)S(1)}, f32[16,4096]{1,0:T(8,128)}, u32[]{:S(2)}) copy-start(f32[16,4096]{1,0:T(8,128)} %shard_map.119) | copy-start | bytes 786436
  322.1 36.9 %all-to-all-start.1 = ((bf16[32,8,4096]{2,1,0:T(8,128)(2,1)}), bf16[32,8,4096]{2,1,0:T(8,128)(2,1)}, u32[]{:S(2)}, u32[]{:S(2)}) async-start(bf16[32,8,4096]{2,1,0:T(8,128)(2,1)} %select_select_fusion), calls=%async_computation.1 | async-start | bytes 4194304 | tf_op jit(solution)/shard_map/all_to_all | solution.py:508
where the time goes:
time: 374 us; the launch traced here: 367 us
  Pallas kernels  240 us (64%)
  other arithmetic  28.8 us (8%)
  waiting for transfers between devices  28.3 us (8%)
  matrix products  27.9 us (7%)
  local copies, waits for them, and re-layouts  22.7 us (6%)
  starting transfers between devices  18.9 us (5%)
    pallas_call x2, Pallas kernels, reduce_scatter_kernel(): pl.pallas_call(functools.partial(_rs_kernel, n, ny), out_shape=jax.ShapeD...  108 us
    pallas_call x1, Pallas kernels, all_gather_two_way(): pl.pallas_call(functools.partial(_ag2_kernel, n, ny), out_shape=(jax.Shap...  84.1 us
    pallas_call x1, Pallas kernels, all_gather_kernel(): pl.pallas_call(functools.partial(_ag_kernel, n, ny), out_shape=jax.ShapeD...  47.5 us
    all_to_all x1, waiting for transfers between devices, body(): lax.all_to_all(back, GROUP, 0, 0, tiled=True)  28.3 us
    all_to_all x1, starting transfers between devices, body(): got = lax.all_to_all(send, GROUP, 0, 0, tiled=True)  11.9 us
  transfers between devices with their start and end apart: 2, of which 1 were waited for; matrix products, arithmetic and copies ran while one was open for 5% of the time, Pallas kernels for 0%

commit v1 on v0

--- a/solution.py
+++ b/solution.py
@@ -308,29 +308,32 @@
         peer = lax.rem(me_y + shift, ny)
         to_y(shift, x_ref.at[pl.ds(0, r)], out1.at[me, peer], y1_send, y1_recv, peer).wait_recv()
 
-    def ring1(d, step, idx):
+    def ring1(d, step, k, idx):
         rows_here = pl.ds(d * half, half)
+        blocks = pl.ds(k * (ny // SUB_CHUNKS), ny // SUB_CHUNKS)
         return pltpu.make_async_remote_copy(
-            src_ref=out1.at[idx, :, rows_here],
-            dst_ref=out1.at[idx, :, rows_here],
-            send_sem=z1_send.at[d, step],
-            recv_sem=z1_recv.at[d, step],
+            src_ref=out1.at[idx, blocks, rows_here],
+            dst_ref=out1.at[idx, blocks, rows_here],
+            send_sem=z1_send.at[d, step, k],
+            recv_sem=z1_recv.at[d, step, k],
             device_id={"cz": dest[d]},
             device_id_type=MESH_ID,
         )
 
     for step in range(n - 1):
+        for k in range(SUB_CHUNKS):
+            for d in range(2):
+                if step > 0:
+                    got = lax.rem(me + n - step, n) if d == 0 else lax.rem(me + step, n)
+                    ring1(d, step - 1, k, got).wait_recv()
+                idx = lax.rem(me + n - step, n) if d == 0 else lax.rem(me + step, n)
+                copy = ring1(d, step, k, idx)
+                copy.start()
+                sends.append(copy)
+    for k in range(SUB_CHUNKS):
         for d in range(2):
-            if step > 0:
-                got = lax.rem(me + n - step, n) if d == 0 else lax.rem(me + step, n)
-                ring1(d, step - 1, got).wait_recv()
-            idx = lax.rem(me + n - step, n) if d == 0 else lax.rem(me + step, n)
-            copy = ring1(d, step, idx)
-            copy.start()
-            sends.append(copy)
-    for d in range(2):
-        got = lax.rem(me + 1, n) if d == 0 else lax.rem(me + n - 1, n)
-        ring1(d, n - 2, got).wait_recv()
+            got = lax.rem(me + 1, n) if d == 0 else lax.rem(me + n - 1, n)
+            ring1(d, n - 2, k, got).wait_recv()
     for shift in range(1, ny):
         peer = lax.rem(me_y + shift, ny)
         to_y(shift, out2.at[me_y], out2.at[peer], y2_send, y2_recv, peer).wait_recv()
@@ -353,8 +356,8 @@
             pltpu.SemaphoreType.DMA((2,)),
             pltpu.SemaphoreType.DMA((ny - 1,)),
             pltpu.SemaphoreType.DMA((ny,)),
-            pltpu.SemaphoreType.DMA((2, n - 1)),
-            pltpu.SemaphoreType.DMA((2, n - 1)),
+            pltpu.SemaphoreType.DMA((2, n - 1, SUB_CHUNKS)),
+            pltpu.SemaphoreType.DMA((2, n - 1, SUB_CHUNKS)),
             pltpu.SemaphoreType.DMA((2, n - 1)),
             pltpu.SemaphoreType.DMA((2, n - 1)),
             pltpu.SemaphoreType.DMA((ny - 1,)),

time: 374 us -> 379 us (1.013)
  waiting for transfers between devices: 28.3 us -> 39.9 us
  starting transfers between devices: 18.9 us -> 14.2 us
    all_to_all x1, waiting for transfers between devices: 28.3 us -> 39.9 us  [body(): lax.all_to_all(back, GROUP, 0, 0, tiled=True)]
    pallas_call x1, Pallas kernels: 47.5 us -> 52.5 us  [all_gather_kernel(): pl.pallas_call(functools.partial(_ag_kernel, n, ny), out_shape=jax.ShapeD...]
    all_to_all x1, starting transfers between devices: 11.9 us -> 7.77 us  [body(): got = lax.all_to_all(send, GROUP, 0, 0, tiled=True)]
    pallas_call x1, Pallas kernels: 84.1 us -> 80 us  [all_gather_two_way(): pl.pallas_call(functools.partial(_ag2_kernel, n, ny), out_shape=(jax.Shap...]
where the time goes in v1:
time: 379 us; the launch traced here: 371 us
  Pallas kernels  237 us (63%)
  waiting for transfers between devices  39.9 us (11%)
  other arithmetic  29 us (8%)
  matrix products  27.9 us (7%)
  local copies, waits for them, and re-layouts  22.7 us (6%)
  starting transfers between devices  14.2 us (4%)
    pallas_call x2, Pallas kernels, reduce_scatter_kernel(): pl.pallas_call(functools.partial(_rs_kernel, n, ny), out_shape=jax.ShapeD...  105 us
    pallas_call x1, Pallas kernels, all_gather_two_way(): pl.pallas_call(functools.partial(_ag2_kernel, n, ny), out_shape=(jax.Shap...  80 us
    pallas_call x1, Pallas kernels, all_gather_kernel(): pl.pallas_call(functools.partial(_ag_kernel, n, ny), out_shape=jax.ShapeD...  52.5 us
    all_to_all x1, waiting for transfers between devices, body(): lax.all_to_all(back, GROUP, 0, 0, tiled=True)  39.9 us
    all_to_all x1, starting transfers between devices, body(): got = lax.all_to_all(send, GROUP, 0, 0, tiled=True)  7.77 us
  transfers between devices with their start and end apart: 2, of which 1 were waited for; matrix products, arithmetic and copies ran while one was open for 5% of the time, Pallas kernels for 0%

profile of v1, /device:TPU:32, one launch (start us, length us, event | category | flops | bytes accessed | tf_op | source)
XLA Modules:
  0.0 371.5 jit_solution(9875417248500845864)
XLA Ops:
  3.6 2.3 gather_fusion
  6.8 80.0 %shard_map.118 = (bf16[8,4,16,4224]{3,2,1,0:T(8,128)(2,1)}, bf16[4,8,16,4224]{3,2,1,0:T(8,128)(2,1)}) custom-call(bf16[32,4224]{1,0:T(8,128)(2,1)} %pad_maximum_fusion.5.x_ref), custom_call_target="tpu_custom_call" | custom-call | tf_op jit(solution)/shard_map/pallas_call | solution.py:347
  86.9 3.2 fusion.3
  90.1 3.1 fusion
  93.3 4.7 %fusion.2 = (bf16[512,4096]{1,0:T(8,128)(2,1)S(1)}, bf16[512,4096]{1,0:T(8,128)(2,1)S(1)}) fusion(f32[4096]{0:T(1024)S(1)} %copy-done.9, f32[512]{0:T(512)S(1)} %add_rsqrt_fusion.1, bf16[512,4224]{1,0:T(8,128)(2,1)} %bitcast.41, f32[512]{0:T(512)S(1)} %add_rsqrt_fusion, bf16[512,4224]{1,0:T(8,128)(2,1)S(1)} %bitcast.39), kind=kLoop, calls=%fused_computation.10 | loop fusion | flops 16777216 | bytes 16797696 | tf_op jit(solution)/shard_map/convert_element_type | solution.py:432
  98.0 2.7 fusion.15
  102.3 7.8 %all-to-all-start = ((bf16[32,2,4,1024]{3,2,1,0:T(4,128)(2,1)}), bf16[32,2,4,1024]{3,2,1,0:T(4,128)(2,1)}, u32[]{:S(2)}, u32[]{:S(2)}) async-start(bf16[32,2,4,1024]{3,2,1,0:T(4,128)(2,1)} %bitcast.11), calls=%async_computation | async-start | bytes 1048576 | tf_op jit(solution)/shard_map/all_to_all | solution.py:447
  113.7 2.9 fusion.55
  116.6 2.9 convolution_add_fusion
  120.5 7.4 %fusion.7 = f32[1024,128]{0,1:T(8,128)} fusion(bf16[4096,128]{1,0:T(8,128)(2,1)} %param.16, bf16[512,4096]{1,0:T(8,128)(2,1)} %copy-done.6, bf16[512,4096]{1,0:T(8,128)(2,1)} %copy-done.5), kind=kOutput, calls=%fused_computation.17 | convolution fusion | flops 1090519040 | bytes 9961472 | tf_op jit(solution)/shard_map/dot_general | solution.py:437
  127.9 2.0 slice_convert_fusion
  129.8 2.0 reshape.690
  132.6 2.8 fusion.33
  139.3 4.7 %fusion.14 = bf16[512,128]{1,0:T(8,128)(2,1)} fusion(s32[512]{0:T(512)S(1)} %eq.146, bf16[128,1024]{1,0:T(8,128)(2,1)S(1)} %copy-done.7, f32[1024,1024]{0,1:T(8,128)} %copy-done.3, f32[1024]{0:T(1024)S(1)} %fusion.8, f32[1024]{0:T(1024)S(1)} %get-tuple-element.29, s32[1024]{0:T(1024)S(1)} %get-tuple-element.13), kind=kOutput, calls=%fused_computation.30 | convolution fusion | flops 409665536 | bytes 4601856 | tf_op jit(solution)/shard_map/dot_general | solution.py:477
  144.0 54.3 %shard_map.119 = f32[16,4096]{1,0:T(8,128)} custom-call(bf16[8,64,128]{2,1,0:T(8,128)(2,1)} %bitcast.49, bf16[128,4096]{1,0:T(8,128)(2,1)} %w_ref.2), custom_call_target="tpu_custom_call" | custom-call | tf_op jit(solution)/shard_map/pallas_call | solution.py:141
  201.2 52.5 %shard_map.120 = bf16[8,4,16,4096]{3,2,1,0:T(8,128)(2,1)} custom-call(bf16[16,4096]{1,0:T(8,128)(2,1)} %multiply_convert_fusion.x_ref), custom_call_target="tpu_custom_call" | custom-call | tf_op jit(solution)/shard_map/pallas_call | solution.py:229
  253.7 4.0 %fusion.125 = f32[512,352]{0,1:T(8,128)S(1)} fusion(bf16[512,4096]{1,0:T(8,128)(2,1)} %bitcast.44, bf16[4096,352]{0,1:T(8,128)(2,1)S(1)} %copy-done), kind=kOutput, calls=%fused_computation.252 | convolution fusion | flops 1476395008 | bytes 7798784 | tf_op jit(solution)/shard_map/dot_general | solution.py:494
  258.1 2.5 fusion.12
  260.5 1.9 copy.45
  262.5 50.3 %shard_map.121 = f32[16,4096]{1,0:T(8,128)} custom-call(bf16[8,64,352]{2,1,0:T(8,128)(2,1)} %bitcast.47, bf16[352,4096]{1,0:T(8,128)(2,1)} %w_ref.3), custom_call_target="tpu_custom_call" | custom-call | tf_op jit(solution)/shard_map/pallas_call | solution.py:141
  315.7 6.4 %all-to-all-start.1 = ((bf16[32,8,4096]{2,1,0:T(8,128)(2,1)}), bf16[32,8,4096]{2,1,0:T(8,128)(2,1)}, u32[]{:S(2)}, u32[]{:S(2)}) async-start(bf16[32,8,4096]{2,1,0:T(8,128)(2,1)} %select_select_fusion), calls=%async_computation.1 | async-start | bytes 4194304 | tf_op jit(solution)/shard_map/all_to_all | solution.py:511
  323.7 39.9 %all-to-all-done.1 = bf16[32,8,4096]{2,1,0:T(8,128)(2,1)} async-done(((bf16[32,8,4096]{2,1,0:T(8,128)(2,1)}), bf16[32,8,4096]{2,1,0:T(8,128)(2,1)}, u32[]{:S(2)}, u32[]{:S(2)}) %all-to-all-start.1) | async-done | bytes 2097184 | tf_op jit(solution)/shard_map/all_to_all | solution.py:511
  363.5 5.0 %gather_fusion.3 = bf16[128,4096]{1,0:T(8,128)(2,1)} fusion(bf16[256,4096]{1,0:T(8,128)(2,1)} %bitcast.16, s32[1024]{0:T(1024)S(1)} %pad_clamp_fusion), kind=kCustom, calls=%fused_computation.3 | custom fusion | bytes 2097664 | tf_op jit(solution)/shard_map/gather | solution.py:518
  368.6 2.7 broadcast_select_fusion
  (94 shorter events, 22.8 us)
Async XLA Ops:
  0.0 253.7 %copy-start = (bf16[4096,352]{0,1:T(8,128)(2,1)S(1)}, bf16[4096,352]{0,1:T(8,128)(2,1)}, u32[]{:S(2)}) copy-start(bf16[4096,352]{0,1:T(8,128)(2,1)} %param.21) | copy-start | bytes 8650756
  86.8 6.4 %copy-start.1 = (bf16[4,8,16,4224]{3,2,1,0:T(8,128)(2,1)S(1)}, bf16[4,8,16,4224]{3,2,1,0:T(8,128)(2,1)}, u32[]{:S(2)}) copy-start(bf16[4,8,16,4224]{3,2,1,0:T(8,128)(2,1)} %get-tuple-element.8) | copy-start | bytes 12976132
  86.9 6.4 %copy-start.9 = (f32[4096]{0:T(1024)S(1)}, f32[4096]{0:T(1024)}, u32[]{:S(2)}) copy-start(f32[4096]{0:T(1024)} %param.15) | copy-start | bytes 49156
  93.2 4.7 %copy-start.11 = (bf16[4096,32]{0,1:T(8,128)(2,1)S(1)}, bf16[4096,32]{0,1:T(8,128)(2,1)}, u32[]{:S(2)}) copy-start(bf16[4096,32]{0,1:T(8,128)(2,1)} %param.18) | copy-start | bytes 786436
  93.2 4.7 %copy-start.12 = (bf16[4096,32]{0,1:T(8,128)(2,1)S(1)}, bf16[4096,32]{0,1:T(8,128)(2,1)}, u32[]{:S(2)}) copy-start(bf16[4096,32]{0,1:T(8,128)(2,1)} %param.17) | copy-start | bytes 786436
  97.9 2.7 copy-start.5
  97.9 3.2 copy-start.6
  102.3 25.6 %all-to-all-start = ((bf16[32,2,4,1024]{3,2,1,0:T(4,128)(2,1)}), bf16[32,2,4,1024]{3,2,1,0:T(4,128)(2,1)}, u32[]{:S(2)}, u32[]{:S(2)}) async-start(bf16[32,2,4,1024]{3,2,1,0:T(4,128)(2,1)} %bitcast.11), calls=%async_computation | async-start | bytes 1048576 | tf_op jit(solution)/shard_map/all_to_all | solution.py:447
  135.5 3.8 %copy-start.7 = (bf16[128,1024]{1,0:T(8,128)(2,1)S(1)}, bf16[128,1024]{1,0:T(8,128)(2,1)}, u32[]{:S(2)}) copy-start(bf16[128,1024]{1,0:T(8,128)(2,1)} %reshape_squeeze.8) | copy-start | bytes 786436
  136.3 1.9 copy-start.3
  139.3 60.2 %copy-start.8 = (f32[4096]{0:T(1024)S(1)}, f32[4096]{0:T(1024)}, u32[]{:S(2)}) copy-start(f32[4096]{0:T(1024)} %param.20) | copy-start | bytes 49156
  253.7 4.0 %copy-start.4 = (bf16[8,4,16,4096]{3,2,1,0:T(8,128)(2,1)S(1)}, bf16[8,4,16,4096]{3,2,1,0:T(8,128)(2,1)}, u32[]{:S(2)}) copy-start(bf16[8,4,16,4096]{3,2,1,0:T(8,128)(2,1)} %shard_map.120) | copy-start | bytes 12582916
  253.7 4.3 %copy-start.10 = (bf16[4096,352]{0,1:T(8,128)(2,1)S(1)}, bf16[4096,352]{0,1:T(8,128)(2,1)}, u32[]{:S(2)}) copy-start(bf16[4096,352]{0,1:T(8,128)(2,1)} %param.22) | copy-start | bytes 8650756
  260.5 52.2 %copy-start.2 = (f32[16,4096]{1,0:T(8,128)S(1)}, f32[16,4096]{1,0:T(8,128)}, u32[]{:S(2)}) copy-start(f32[16,4096]{1,0:T(8,128)} %shard_map.119) | copy-start | bytes 786436
  315.7 47.9 %all-to-all-start.1 = ((bf16[32,8,4096]{2,1,0:T(8,128)(2,1)}), bf16[32,8,4096]{2,1,0:T(8,128)(2,1)}, u32[]{:S(2)}, u32[]{:S(2)}) async-start(bf16[32,8,4096]{2,1,0:T(8,128)(2,1)} %select_select_fusion), calls=%async_computation.1 | async-start | bytes 4194304 | tf_op jit(solution)/shard_map/all_to_all | solution.py:511
